TPU v7x, 32 devices: a whole 2x2x4 slice. The times are simulated.
32 devices in a mesh: lines: 8 (over z, x), temp: 4 (over y, core).
Axes of the slice: x: 2, y: 2, z: 4, core: 2. Of those that a mesh axis runs over, the one named last changes fastest.
Arguments:
- line_position: float32 [384, 128], P('lines'), may hold values from 0 to 256
- line_strength: float32 [384, 128], P('lines'), may hold values from 0.05 to 1
- lower_energy: float32 [384, 128], P('lines'), may hold values from 0 to 1500
- broad_width: float32 [384, 128], P('lines'), may hold values from 0.3 to 3
- broad_exponent: float32 [384, 128], P('lines'), may hold values from 0.3 to 1
- doppler_width: float32 [384, 128], P('lines'), may hold values from 0.3 to 3
- block_window: int32 [384], P('lines'), may hold values from 0 to 31, as said below
- tile_offset: int32 [384], P('lines'), may hold values from 0 to 1792
- owner_slot: int32 [32], replicated, may hold values from 0 to 31, as said below
Outputs:
- polynomial_weights: float32 [8, 32, 2048], P('temp', 'lines')
Inputs may be any that keep to these rules, and one draw needn't show every extreme that they name: owner_slot is a permutation of the 32 window places. `block_window`: of the 48 blocks of one index of lines, exactly 12 fall on windows of each of 2 owners and 4 on windows of each other owner; some owner receives 12 blocks from every index of lines.
All inputs are finite; a program needn't handle non-finite values.
Results may differ from a plain program's by a relative error of at most 0.00015.
Values sent between devices are 32-bit elements; how exact they have to be, the bound alone decides.
No kernel may reach another device: no remote copies, remote signals or barrier semaphores. Data moves between devices by JAX's collectives and lax.ppermute only.
A program may use at most 128 MiB of HBM per device.

v0:
```python
import math

import jax
import jax.numpy as jnp
from jax import lax
from jax.sharding import PartitionSpec as P

LINES_BLK = 128
PATCH_SAMPLES = 256
SPAN_SAMPLES = 2048
THERMAL_SAMPLES = 8


REFERENCE_KELVIN = 1000.0


def thermal_abscissae(line_count):
    theta = math.pi * (jnp.arange(line_count, dtype=jnp.float32) + 0.5) / line_count
    return 1650.0 + 1350.0 * jnp.cos(theta)


def polynomial_regression(line_count):
    order = jnp.arange(line_count, dtype=jnp.float32)
    theta = math.pi * (jnp.arange(line_count, dtype=jnp.float32) + 0.5) / line_count
    factor = jnp.where(order == 0.0, 1.0 / line_count, 2.0 / line_count)
    return factor[:, None] * jnp.cos(order[:, None] * theta[None, :])


def shape_function_piece(
    transition_position,
    base_intensity,
    lower_level_term,
    collisional_broadening_base,
    collisional_power_law,
    thermal_broadening_scale,
    kelvin_value,
    wavenumber_points,
):
    reciprocal_kelvin = 1.0 / kelvin_value
    temp_ratio = REFERENCE_KELVIN * reciprocal_kelvin
    scaled = base_intensity * jnp.exp(
        -lower_level_term * (reciprocal_kelvin - 1.0 / REFERENCE_KELVIN)
    )
    lorentz_width = (
        2.0 * collisional_broadening_base * jnp.exp(collisional_power_law * jnp.log(temp_ratio))
    )
    gaussian_halfwidth = (
        2.35482 * thermal_broadening_scale * jnp.sqrt(kelvin_value / REFERENCE_KELVIN)
    )
    gw, lw = (gaussian_halfwidth, lorentz_width)
    full_width = (
        gw**5
        + 2.69269 * gw**4 * lw
        + 2.42843 * gw**3 * lw**2
        + 4.47163 * gw**2 * lw**3
        + 0.07842 * gw * lw**4
        + lw**5
    ) ** 0.2
    share = lw / full_width
    mixing = 1.36603 * share - 0.47719 * share**2 + 0.11116 * share**3
    grid_points = jnp.arange(wavenumber_points, dtype=jnp.float32) + 0.5
    distance = grid_points - transition_position[..., None]
    half_width = 0.5 * full_width[..., None]
    lorentz = half_width / (math.pi * (distance * distance + half_width * half_width))
    wide = full_width[..., None]
    gaussian = 0.939437 / wide * jnp.exp(-2.7725887 * distance * distance / (wide * wide))
    mixed = mixing[..., None]
    return jnp.sum(scaled[..., None] * (mixed * lorentz + (1.0 - mixed) * gaussian), axis=-2)


def compute_partitions(record_columns, thermal_readings):
    line_count = record_columns[0].shape[0]
    group = math.gcd(16, line_count)
    thermal_tally = thermal_readings.shape[0]
    grouped = tuple((a.reshape(line_count // group, group, LINES_BLK) for a in record_columns))

    def evaluate(pieces):
        (
            transition_position,
            base_intensity,
            lower_level_term,
            collisional_broadening_base,
            collisional_power_law,
            thermal_broadening_scale,
        ) = pieces
        return jnp.stack(
            [
                shape_function_piece(
                    transition_position,
                    base_intensity,
                    lower_level_term,
                    collisional_broadening_base,
                    collisional_power_law,
                    thermal_broadening_scale,
                    thermal_readings[thermal_position],
                    PATCH_SAMPLES,
                )
                for thermal_position in range(thermal_tally)
            ]
        )

    stacked = lax.map(evaluate, grouped)
    return jnp.moveaxis(stacked, 1, 0).reshape(thermal_tally, line_count, PATCH_SAMPLES)


def on_device(
    line_position,
    line_strength,
    lower_energy,
    broad_width,
    broad_exponent,
    doppler_width,
    block_window,
    tile_offset,
    owner_slot,
):
    lines_n = lax.axis_size("lines")
    thermal_number = lax.axis_size("temp")
    spectral_intervals = owner_slot.shape[0]
    by_holder = spectral_intervals // lines_n
    thermal_portion = THERMAL_SAMPLES // thermal_number
    primary_thermal_sample = lax.axis_index("temp") * thermal_portion
    record_columns = (
        line_position,
        line_strength,
        lower_energy,
        broad_width,
        broad_exponent,
        doppler_width,
    )
    matches = block_window[:, None] == jnp.arange(spectral_intervals, dtype=jnp.int32)[None, :]
    slot_index = jnp.sum(jnp.where(matches, owner_slot[None, :], 0), axis=1)
    tile_span = jnp.arange(PATCH_SAMPLES, dtype=jnp.int32)
    regression_matrix = polynomial_regression(THERMAL_SAMPLES)
    resident_thermal_samples = lax.dynamic_slice_in_dim(
        thermal_abscissae(THERMAL_SAMPLES), primary_thermal_sample, thermal_portion
    )
    patch_entries = compute_partitions(record_columns, resident_thermal_samples)
    flat_index = (slot_index * SPAN_SAMPLES + tile_offset)[:, None] + tile_span[None, :]
    local_sum = (
        jnp.zeros((thermal_portion, spectral_intervals * SPAN_SAMPLES), jnp.float32)
        .at[:, flat_index]
        .add(patch_entries)
    )
    absorption_curves = lax.psum_scatter(local_sum, "lines", scatter_dimension=1, tiled=True)
    all_spectra = lax.all_gather(absorption_curves, "temp", axis=0, tiled=True)
    regression_equations = lax.dynamic_slice_in_dim(
        regression_matrix, primary_thermal_sample, thermal_portion, 0
    )
    polynomial_weights = jnp.dot(
        regression_equations,
        all_spectra,
        precision=lax.Precision.HIGHEST,
        preferred_element_type=jnp.float32,
    )
    return polynomial_weights.reshape(thermal_portion, by_holder, SPAN_SAMPLES)


def solution(mesh):
    return jax.shard_map(
        on_device,
        mesh=mesh,
        in_specs=(
            P("lines", None),
            P("lines", None),
            P("lines", None),
            P("lines", None),
            P("lines", None),
            P("lines", None),
            P("lines"),
            P("lines"),
            P(),
        ),
        out_specs=P("temp", "lines", None),
        check_vma=False,
    )
```

profile of v0, /device:TPU:0, one launch (start us, length us, event | category | flops | bytes accessed | tf_op | source)
XLA Modules:
  0.0 677.5 jit_solution(3638820215308285592)
XLA Ops:
  6.5 0.0 reduce-scatter.2.cloned.1.call-start
  6.6 0.1 dynamic_slice.50
  6.7 0.6 fusion.65
  10.1 21.4 %while.13 = (s32[]{:T(128)}, f32[3,2,16,256]{3,2,0,1:T(8,128)S(1)}, f32[3,16,128]{2,1,0:T(8,128)}, f32[3,16,128]{2,1,0:T(8,128)}, f32[]{:T(128)}, /*index=5*/f32...) while((s32[]{:T(128)}, f32[3,2,16,256]{3,2,0,1:T(8,128)S(1)}, ...), condition=%wide.region_4.5_spmd, body=%wide.region_1.4_spmd.sunk | while | flops 12761346 | bytes 444605 | solution.py:102
  10.1 0.8 power_multiply_fusion.7
  10.9 0.8 fusion.70
  11.6 0.7 multiply_bitcast_fusion.3
  12.4 4.8 fusion.71
  17.2 0.8 power_multiply_fusion.7
  18.0 0.8 fusion.70
  18.8 0.7 multiply_bitcast_fusion.3
  19.5 4.8 fusion.71
  24.4 0.8 power_multiply_fusion.7
  25.2 0.8 fusion.70
  25.9 0.7 multiply_bitcast_fusion.3
  26.7 4.8 fusion.71
  31.5 0.0 copy-start
  31.5 0.0 copy-start.1
  31.5 0.0 copy-start.2
  31.5 3.9 copy.19
  35.5 0.0 copy-done
  35.5 0.0 copy-done.1
  35.5 0.1 select_reduce_fusion
  35.6 0.0 copy-done.2
  35.6 0.1 fusion.57
  35.7 79.1 %scatter_custom_fusion = f32[2,65536]{0,1:T(8,128)} fusion(s32[12288]{0:T(1024)S(1)} %bitcast.83, f32[12288,2]{1,0:T(8,128)} %bitcast.72, f32[]{:T(128)} %constant.175.clone.1), kind=kCustom, calls=%fused_computation.96 | custom fusion | flops 24576 | bytes 524800 | tf_op jit(solution)/shard_map/scatter-add | solution.py:143
  114.8 0.0 reduce-scatter.2.cloned.1.call-update
  114.9 0.1 cosine_multiply_fusion
  114.9 545.9 %reduce-scatter.2.cloned.1.call-done = f32[2,8192]{0,1:T(8,128)} async-done(((f32[2,65536]{0,1:T(8,128)}), f32[2,8192]{0,1:T(8,128)}) %reduce-scatter.2.cloned.1.call-update) | async-done | bytes 65552 | tf_op jit(solution)/shard_map/reduce_scatter | solution.py:145
  660.8 2.8 copy.18
  663.6 5.8 all-gather
  669.4 0.2 reshape.518
  669.6 0.4 fusion.58
  670.0 0.7 reshape.507
  (11 shorter events, 0.1 us)
Async XLA Ops:
  6.5 654.2 %reduce-scatter.2.cloned.1.call-start = ((), (), s32[]{:S(2)}) async-start(), calls=%async_computation.1 | async-start | bytes 37748736 | tf_op jit(solution)/shard_map/reduce_scatter | solution.py:145
  31.5 4.0 copy-start
  31.5 3.9 copy-start.1
  31.5 4.0 copy-start.2
Sparse Core Ops, SparseCore 0:
  115.0 545.7 reduce-scatter.1
where the time goes:
time: 679 us; the launch traced here: 677 us
  waiting for transfers between devices  546 us (80%)
  other arithmetic  101 us (15%)
  between operations  16.3 us (2%)
  local copies, waits for them, and re-layouts  8.37 us (1%)
    reduce_scatter x1, waiting for transfers between devices, on_device(): lax.psum_scatter(local_sum, 'lines', scatter_dimension=1, tiled=True)  546 us
    scatter-add x1, other arithmetic, on_device(): local_sum = jnp.zeros((thermal_portion, spectral_intervals * SPAN_SAMPLES...  79.1 us
    reduce_sum x3, other arithmetic, shape_function_piece(): jnp.sum(scaled[..., None] * (mixed * lorentz + (1.0 - mixed) * gaussian),...  14.4 us
  transfers between devices with their start and end apart: 1, of which 1 were waited for; matrix products, arithmetic and copies ran while one was open for 0% of the time, Pallas kernels for 0%

commit v1 on v0

v1 whole, which is shorter than its diff:
```python
import functools
import math

import jax
import jax.numpy as jnp
import numpy as np
from jax import lax
from jax.experimental import pallas as pl
from jax.experimental.pallas import tpu as pltpu
from jax.sharding import PartitionSpec as P

LANES = 128
ROWS = 8
PATCH_SAMPLES = 256
SPAN_SAMPLES = 2048
THERMAL_SAMPLES = 8
REFERENCE_KELVIN = 1000.0
PACK = 4
PIECE = LANES // PACK
SEATS = 16
HIGHEST = lax.Precision.HIGHEST


def kelvins():
    theta = math.pi * (np.arange(THERMAL_SAMPLES) + 0.5) / THERMAL_SAMPLES
    return [float(k) for k in 1650.0 + 1350.0 * np.cos(theta)]


def regression():
    order = np.arange(THERMAL_SAMPLES)
    theta = math.pi * (np.arange(THERMAL_SAMPLES) + 0.5) / THERMAL_SAMPLES
    factor = np.where(order == 0, 1.0, 2.0) / THERMAL_SAMPLES
    return factor[:, None] * np.cos(order[:, None] * theta[None, :])


class Plan:
    def __init__(self, lines_n, temp_n, blocks, spans):
        self.lines_n, self.temp_n, self.blocks, self.spans = lines_n, temp_n, blocks, spans
        self.held = spans // lines_n
        self.orders = THERMAL_SAMPLES // temp_n
        self.share = -(-blocks // temp_n)
        self.quads = -(-self.share // PACK)
        heavy = 3 * ((2 * blocks) // (3 * lines_n))
        self.cap = -(-heavy // temp_n)
        self.data_rows = self.cap * self.orders
        self.rows = -(-(self.data_rows + (self.cap + 1) // 2) // ROWS) * ROWS
        self.depth = THERMAL_SAMPLES * SEATS + 2 * SEATS
        assert self.share <= SEATS and self.orders * self.held <= ROWS

    def tables(self):
        fit = regression()
        weight = np.zeros((self.temp_n, self.rows, self.depth), np.float32)
        place = np.full((self.temp_n, self.rows, self.depth), -1.0, np.float32)
        tile_columns = THERMAL_SAMPLES * SEATS
        for device in range(self.temp_n):
            for slot in range(self.cap):
                for order in range(self.orders):
                    row = slot * self.orders + order
                    for t in range(THERMAL_SAMPLES):
                        cells = slice(t * SEATS, (t + 1) * SEATS)
                        weight[device, row, cells] = fit[device * self.orders + order, t]
                        place[device, row, cells] = slot
                row = self.data_rows + slot // 2
                start = tile_columns + (slot % 2) * SEATS
                weight[device, row, start : start + SEATS] = 1.0
                place[device, row, start : start + SEATS] = slot
        both = np.stack([weight, place])
        return both.reshape(2, self.temp_n * self.rows, self.depth)


def line_terms(strength, energy, broad, power, doppler, kelvin):
    inverse = 1.0 / kelvin
    scaled = strength * jnp.exp(energy * (1.0 / REFERENCE_KELVIN - inverse))
    lw = 2.0 * broad * jnp.exp(power * math.log(REFERENCE_KELVIN * inverse))
    gw = (2.35482 * math.sqrt(kelvin / REFERENCE_KELVIN)) * doppler
    g2, l2 = gw * gw, lw * lw
    g3, l3 = g2 * gw, l2 * lw
    g4, l4 = g2 * g2, l2 * l2
    total = (
        g4 * gw
        + 2.69269 * g4 * lw
        + 2.42843 * g3 * l2
        + 4.47163 * g2 * l3
        + 0.07842 * gw * l4
        + l4 * lw
    )
    full = jnp.exp(0.2 * jnp.log(total))
    narrow = 1.0 / full
    share = lw * narrow
    mixing = share * (1.36603 + share * (-0.47719 + share * 0.11116))
    half = 0.5 * full
    lorentz = scaled * mixing * half * (1.0 / math.pi)
    gauss = scaled * (1.0 - mixing) * (0.939437 * narrow)
    slope = (-2.7725887 * math.log2(math.e)) * narrow * narrow
    return half * half, lorentz, slope, gauss


def tile_kernel(
    plan,
    position,
    strength,
    energy,
    broad,
    power,
    doppler,
    window,
    offset,
    owner_slot,
    table,
    sent,
    terms,
    squares,
    mixed,
    tiles,
):
    blocks, temp_n = plan.blocks, plan.temp_n
    me = lax.axis_index("temp").astype(jnp.float32)
    f32 = jnp.float32

    def iota(shape, axis):
        return lax.broadcasted_iota(jnp.int32, shape, axis).astype(f32)

    down, across = iota((blocks, blocks), 0), iota((blocks, blocks), 1)
    eye = down == across

    def stand(row):
        return jnp.sum(jnp.where(eye, row, 0.0), axis=1, keepdims=True)

    def lay(column):
        return jnp.sum(jnp.where(eye, column, 0.0), axis=0, keepdims=True)

    window_column = stand(window[...].astype(f32))
    offset_column = stand(offset[...].astype(f32))
    seat = owner_slot[...].astype(f32)
    slot_column = jnp.sum(
        jnp.where(window_column == iota((blocks, plan.spans), 1), seat, 0.0), axis=1, keepdims=True
    )
    owner_column = jnp.floor((slot_column + 0.5) * (1.0 / plan.held))
    owner_row = lay(owner_column)
    begin_column = (slot_column - owner_column * plan.held) * SPAN_SAMPLES + offset_column
    key_column = owner_column * blocks + iota((blocks, 1), 0)
    key_row = owner_row * blocks + iota((1, blocks), 1)
    rank_row = jnp.sum(jnp.where(key_column < key_row, 1.0, 0.0), axis=0, keepdims=True)
    rank_column = jnp.sum(jnp.where(key_row < key_column, 1.0, 0.0), axis=1, keepdims=True)

    picks = PACK * ROWS
    pick_row = lax.broadcasted_iota(jnp.int32, (picks, blocks), 0)
    quad, piece = pick_row % ROWS, pick_row // ROWS
    local = quad * PACK + piece
    wanted = (local * temp_n).astype(f32) + me
    fits = (quad < plan.quads) & (local < plan.share)
    pick = jnp.where(fits & (rank_row == wanted), 1.0, 0.0)

    def gather(values):
        return jnp.dot(pick, values, precision=HIGHEST, preferred_element_type=f32)

    lane = lax.broadcasted_iota(jnp.int32, (ROWS, LANES), 1)
    segment = lane // PIECE

    def pack(values):
        parts = [values[i * ROWS : (i + 1) * ROWS] for i in range(PACK)]
        out = []
        for j in range(PACK):
            chosen = parts[0]
            for i in range(1, PACK):
                chosen = jnp.where(segment == (i + j) % PACK, parts[i], chosen)
            out.append(chosen if j == 0 else pltpu.roll(chosen, LANES - j * PIECE, 1))
        return out

    begin = gather(jnp.broadcast_to(begin_column, (blocks, LANES)))
    begin_packed = pack(begin)[0]
    columns = [pack(gather(r[...])) for r in (position, strength, energy, broad, power, doppler)]
    for j in range(PACK):
        for t, kelvin in enumerate(kelvins()):
            for k, value in enumerate(line_terms(*(c[j] for c in columns[1:]), kelvin)):
                terms[t, k * PACK + j] = value

    shift = begin_packed - jnp.floor(begin_packed * (1.0 / LANES)) * LANES
    grid = iota((PATCH_SAMPLES, LANES), 0)
    for q in range(plan.quads):
        point = grid - shift[q : q + 1]
        point = jnp.where(point < 0.0, point + PATCH_SAMPLES, point) + 0.5
        for j in range(PACK):
            distance = point - columns[0][j][q : q + 1]
            squares[j] = distance * distance

        def one(t, carry, q=q):
            row = [terms[t, k, pl.ds(q, 1), :] for k in range(4 * PACK)]
            row = [jnp.broadcast_to(r, (ROWS, LANES)) for r in row]
            half2, lorentz = row[:PACK], row[PACK : 2 * PACK]
            slope, gauss = row[2 * PACK : 3 * PACK], row[3 * PACK :]
            for m in range(0, PATCH_SAMPLES, ROWS):
                square = [squares[j, m : m + ROWS, :] for j in range(PACK)]
                below = [square[j] + half2[j] for j in range(PACK)]
                above = list(lorentz)
                while len(below) > 1:
                    above = [
                        above[i] * below[i + 1] + above[i + 1] * below[i]
                        for i in range(0, len(below), 2)
                    ]
                    below = [below[i] * below[i + 1] for i in range(0, len(below), 2)]
                value = above[0] / below[0]
                for j in range(PACK):
                    value = value + gauss[j] * jnp.exp2(slope[j] * square[j])
                mixed[m : m + ROWS, :] = value
            for half in range(0, PATCH_SAMPLES, LANES):
                turned = jnp.transpose(mixed[half : half + LANES, :])
                summed = jnp.sum(turned.reshape(PACK, PIECE, LANES), axis=1)
                tiles[t, q * PACK : (q + 1) * PACK, half : half + LANES] = summed
            return carry

        lax.fori_loop(0, THERMAL_SAMPLES, one, 0)

    depth = plan.depth
    column = lax.broadcasted_iota(jnp.int32, (blocks, depth), 1) % SEATS
    mine = rank_column == (column * temp_n).astype(f32) + me
    real = column < plan.share
    owner_wide = jnp.sum(jnp.where(mine & real, owner_column, 0.0), axis=0, keepdims=True)
    first_wide = jnp.sum(
        jnp.where(owner_column < owner_wide, 1.0, 0.0), axis=0, keepdims=True
    )
    column_row = lax.broadcasted_iota(jnp.int32, (1, depth), 1) % SEATS
    skipped = jnp.floor((first_wide - me + (temp_n - 0.5)) * (1.0 / temp_n))
    place_wide = owner_wide * plan.cap + column_row.astype(f32) - skipped
    place_wide = jnp.where(column_row < plan.share, place_wide, -2.0)

    begins = jnp.concatenate(
        [begin[(n % PACK) * ROWS + n // PACK :][:1] for n in range(plan.quads * PACK)]
        + [jnp.zeros((SEATS - plan.quads * PACK, LANES), f32)]
    )
    if plan.share < SEATS:
        tiles[:, plan.share :, :] = jnp.zeros(
            (THERMAL_SAMPLES, SEATS - plan.share, PATCH_SAMPLES), f32
        )
    nothing = jnp.zeros_like(begins)
    body = jnp.concatenate(
        [
            tiles[...].reshape(THERMAL_SAMPLES * SEATS, PATCH_SAMPLES),
            jnp.concatenate([begins, nothing], axis=1),
            jnp.concatenate([nothing, begins], axis=1),
        ]
    )
    group = temp_n * plan.rows
    weight, place = table[0], table[1]
    for owner in range(plan.lines_n):
        spread = jnp.where(
            (place >= 0.0) & (place + owner * plan.cap == place_wide), weight, 0.0
        )
        sent[owner * group : (owner + 1) * group, :] = jnp.dot(
            spread, body, precision=HIGHEST, preferred_element_type=f32
        )


def place_kernel(plan, got, out):
    f32 = jnp.float32
    senders = plan.lines_n * plan.temp_n
    chunks = SPAN_SAMPLES // LANES
    shape = (senders, plan.rows, LANES)
    both = got[...].reshape(senders, plan.rows, PATCH_SAMPLES)
    left, right = both[:, :, :LANES], both[:, :, LANES:]
    sub = lax.broadcasted_iota(jnp.int32, shape, 1)
    begin = jnp.zeros(shape, f32)
    for slot in range(plan.cap):
        row = plan.data_rows + slot // 2
        source = (right if slot % 2 else left)[:, row : row + 1, :]
        begin = jnp.where(sub // plan.orders == slot, source, begin)
    chunk = jnp.floor(begin * (1.0 / LANES))
    shift = begin - chunk * LANES
    own = jnp.floor(chunk * (1.0 / chunks))
    order = (sub % plan.orders).astype(f32)
    target = (chunk - own * chunks) * ROWS + order * plan.held + own
    lane = lax.broadcasted_iota(jnp.int32, shape, 2).astype(f32)
    hit = jnp.where((sub < plan.data_rows) & (target == lane), 1.0, 0.0)
    early = lane >= shift
    rows = senders * plan.rows
    spread = jnp.concatenate(
        [
            jnp.where(early, left, 0.0).reshape(rows, LANES),
            right.reshape(rows, LANES),
            jnp.where(early, 0.0, left).reshape(rows, LANES),
        ],
        axis=1,
    )
    landed = lax.dot_general(
        hit.reshape(rows, LANES),
        spread,
        (((0,), (0,)), ((), ())),
        precision=HIGHEST,
        preferred_element_type=f32,
    )
    for c in range(chunks):
        total = landed[c * ROWS : (c + 1) * ROWS, :LANES]
        for back in (1, 2):
            if c >= back:
                total = total + landed[
                    (c - back) * ROWS : (c - back + 1) * ROWS, back * LANES : (back + 1) * LANES
                ]
        for order_at in range(plan.orders):
            out[order_at, :, c * LANES : (c + 1) * LANES] = total[
                order_at * plan.held : (order_at + 1) * plan.held
            ]


def on_device(
    line_position,
    line_strength,
    lower_energy,
    broad_width,
    broad_exponent,
    doppler_width,
    block_window,
    tile_offset,
    owner_slot,
):
    plan = Plan(
        lax.axis_size("lines"),
        lax.axis_size("temp"),
        line_position.shape[0],
        owner_slot.shape[0],
    )
    devices = plan.lines_n * plan.temp_n
    f32 = jnp.float32
    sent = pl.pallas_call(
        functools.partial(tile_kernel, plan),
        out_shape=jax.ShapeDtypeStruct((devices * plan.rows, PATCH_SAMPLES), f32),
        scratch_shapes=[
            pltpu.VMEM((THERMAL_SAMPLES, 4 * PACK, ROWS, LANES), f32),
            pltpu.VMEM((PACK, PATCH_SAMPLES, LANES), f32),
            pltpu.VMEM((PATCH_SAMPLES, LANES), f32),
            pltpu.VMEM((THERMAL_SAMPLES, SEATS, PATCH_SAMPLES), f32),
        ],
        name="tiles",
    )(
        line_position,
        line_strength,
        lower_energy,
        broad_width,
        broad_exponent,
        doppler_width,
        block_window[None, :],
        tile_offset[None, :],
        owner_slot[None, :],
        jnp.asarray(plan.tables()),
    )
    got = lax.all_to_all(
        sent.reshape(devices, plan.rows, PATCH_SAMPLES), ("lines", "temp"), 0, 0, tiled=True
    )
    return pl.pallas_call(
        functools.partial(place_kernel, plan),
        out_shape=jax.ShapeDtypeStruct((plan.orders, plan.held, SPAN_SAMPLES), f32),
        name="place",
    )(got.reshape(devices * plan.rows, PATCH_SAMPLES))


def solution(mesh):
    return jax.shard_map(
        on_device,
        mesh=mesh,
        in_specs=(
            P("lines", None),
            P("lines", None),
            P("lines", None),
            P("lines", None),
            P("lines", None),
            P("lines", None),
            P("lines"),
            P("lines"),
            P(),
        ),
        out_specs=P("temp", "lines", None),
        check_vma=False,
    )
```

time: 679 us -> 29.1 us (0.04)
  waiting for transfers between devices: 546 us -> 0 us
  other arithmetic: 101 us -> 0 us
  between operations: 16.3 us -> 0.01 us
  blocking collectives: 5.79 us -> 18 us
  Pallas kernels: 0 us -> 10.8 us
  local copies, waits for them, and re-layouts: 8.37 us -> 0 us
    reduce_scatter x1 -> x0, waiting for transfers between devices: 546 us -> none  [on_device(): lax.psum_scatter(local_sum, 'lines', scatter_dimension=1, tiled=True)]
    scatter-add x1 -> x0, other arithmetic: 79.1 us -> none  [on_device(): local_sum = jnp.zeros((thermal_portion, spectral_intervals * SPAN_SAMPLES...]
    all_to_all x0 -> x1, blocking collectives: none -> 18 us  [on_device(): lax.all_to_all(sent.reshape(devices, plan.rows, PATCH_SAMPLES), ('lines',...]
    reduce_sum x4 -> x0, other arithmetic: 14.5 us -> none  [the longest x3 14.4 us: shape_function_piece(): jnp.sum(scaled[..., None] * (mixed * lorentz + (1.0 - mixed) * gaussian),...]
    pallas_call x0 -> x2, Pallas kernels: none -> 10.8 us  [the longest x1 8.77 us: on_device(): pl.pallas_call(functools.partial(tile_kernel, plan), out_shape=jax.ShapeD...]
    mul x10 -> x0, other arithmetic: 6.92 us -> none  [the longest x3 2.34 us: shape_function_piece(): half_width = 0.5 * full_width[..., None]]
  transfers between devices with their start and end apart: 1 -> 0, of which waited for: 1 -> 0; matrix products, arithmetic and copies ran while one was open for 0% -> 0% of each run, Pallas kernels for 0% -> 0%
where the time goes in v1:
time: 29.1 us; the launch traced here: 28.8 us
  blocking collectives  18 us (62%)
  Pallas kernels  10.8 us (37%)
    all_to_all x1, blocking collectives, on_device(): lax.all_to_all(sent.reshape(devices, plan.rows, PATCH_SAMPLES), ('lines',...  18 us
    pallas_call x1, Pallas kernels, on_device(): pl.pallas_call(functools.partial(tile_kernel, plan), out_shape=jax.ShapeD...  8.77 us
    pallas_call x1, Pallas kernels, on_device(): pl.pallas_call(functools.partial(place_kernel, plan), out_shape=jax.Shape...  2.07 us

profile of v1, /device:TPU:0, one launch (start us, length us, event | category | flops | bytes accessed | tf_op | source)
XLA Modules:
  0.0 28.8 jit_solution(5108140789889474644)
XLA Ops:
  0.0 8.8 %tiles.1 = f32[256,256]{1,0:T(8,128)} custom-call(f32[48,128]{1,0:T(8,128)} %position.1, f32[48,128]{1,0:T(8,128)} %strength.1, f32[48,128]{1,0:T(8,128)} %energy.1, f32[48,128]{1,0:T(8,128)} %broad.1, f32[48,128]{1,0:T(8,128)} %power.1, f32[48,128]{1,0:T(8,128)} %doppler.1, s32[1,48]{1,0:T(1,128)} %bitcast.7, s32[1,48]{1,0:T(1,128)} %bitcast.8, ...), custom_call_target="tpu_custom_call" | custom-call | tf_op jit(solution)/shard_map/tiles/pallas_call | solution.py:323
  8.8 18.0 %all_to_all.5 = f32[32,8,256]{2,1,0:T(8,128)} all-to-all(f32[32,8,256]{2,1,0:T(8,128)} %bitcast.6), channel_id=1, replica_groups=mesh['lines'=8,'temp'=4] {'lines','temp'}, dimensions={0} | all-to-all | bytes 524288 | tf_op jit(solution)/shard_map/all_to_all | solution.py:345
  26.8 2.1 %place.1 = f32[2,4,2048]{2,1,0:T(4,128)} custom-call(f32[256,256]{1,0:T(8,128)} %bitcast.5), custom_call_target="tpu_custom_call" | custom-call | tf_op jit(solution)/shard_map/place/pallas_call | solution.py:348

commit v2 on v1

--- a/solution.py
+++ b/solution.py
@@ -18,6 +18,7 @@
 PACK = 4
 PIECE = LANES // PACK
 SEATS = 16
+STEP = 16
 HIGHEST = lax.Precision.HIGHEST
 
 
@@ -42,30 +43,18 @@
         self.quads = -(-self.share // PACK)
         heavy = 3 * ((2 * blocks) // (3 * lines_n))
         self.cap = -(-heavy // temp_n)
-        self.data_rows = self.cap * self.orders
-        self.rows = -(-(self.data_rows + (self.cap + 1) // 2) // ROWS) * ROWS
-        self.depth = THERMAL_SAMPLES * SEATS + 2 * SEATS
-        assert self.share <= SEATS and self.orders * self.held <= ROWS
-
-    def tables(self):
-        fit = regression()
-        weight = np.zeros((self.temp_n, self.rows, self.depth), np.float32)
-        place = np.full((self.temp_n, self.rows, self.depth), -1.0, np.float32)
-        tile_columns = THERMAL_SAMPLES * SEATS
-        for device in range(self.temp_n):
-            for slot in range(self.cap):
-                for order in range(self.orders):
-                    row = slot * self.orders + order
-                    for t in range(THERMAL_SAMPLES):
-                        cells = slice(t * SEATS, (t + 1) * SEATS)
-                        weight[device, row, cells] = fit[device * self.orders + order, t]
-                        place[device, row, cells] = slot
-                row = self.data_rows + slot // 2
-                start = tile_columns + (slot % 2) * SEATS
-                weight[device, row, start : start + SEATS] = 1.0
-                place[device, row, start : start + SEATS] = slot
-        both = np.stack([weight, place])
-        return both.reshape(2, self.temp_n * self.rows, self.depth)
+        self.lots = self.cap * self.orders
+        self.rows = 2 * self.lots + 1
+        assert self.share <= SEATS and self.cap <= PACK
+        assert self.orders * self.held <= ROWS and ROWS % temp_n == 0
+
+    def table(self):
+        weight = regression().astype(np.float32)
+        rows = [
+            [weight[(d % self.temp_n) * self.orders + order] for d in range(ROWS)]
+            for order in range(self.orders)
+        ]
+        return np.repeat(np.array(rows), SEATS, axis=2)
 
 
 def line_terms(strength, energy, broad, power, doppler, kelvin):
@@ -147,9 +136,9 @@
     pick_row = lax.broadcasted_iota(jnp.int32, (picks, blocks), 0)
     quad, piece = pick_row % ROWS, pick_row // ROWS
     local = quad * PACK + piece
-    wanted = (local * temp_n).astype(f32) + me
     fits = (quad < plan.quads) & (local < plan.share)
-    pick = jnp.where(fits & (rank_row == wanted), 1.0, 0.0)
+    wanted = jnp.where(fits, (local * temp_n).astype(f32) + me, 0.0)
+    pick = jnp.where(rank_row == wanted, 1.0, 0.0)
 
     def gather(values):
         return jnp.dot(pick, values, precision=HIGHEST, preferred_element_type=f32)
@@ -182,15 +171,25 @@
         point = jnp.where(point < 0.0, point + PATCH_SAMPLES, point) + 0.5
         for j in range(PACK):
             distance = point - columns[0][j][q : q + 1]
-            squares[j] = distance * distance
-
-        def one(t, carry, q=q):
+            squares[q * PACK + j] = distance * distance
+
+    width = 2 * plan.quads * LANES
+    across_lines = lax.broadcasted_iota(jnp.int32, (SEATS, width), 1)
+    seat_of = across_lines // (2 * LANES) * PACK + across_lines % LANES // PIECE
+    seats = jnp.where(
+        (seat_of == lax.broadcasted_iota(jnp.int32, (SEATS, width), 0)) & (seat_of < plan.share),
+        1.0,
+        0.0,
+    ).astype(jnp.bfloat16)
+
+    def one(t, carry):
+        for q in range(plan.quads):
             row = [terms[t, k, pl.ds(q, 1), :] for k in range(4 * PACK)]
-            row = [jnp.broadcast_to(r, (ROWS, LANES)) for r in row]
+            row = [jnp.broadcast_to(r, (STEP, LANES)) for r in row]
             half2, lorentz = row[:PACK], row[PACK : 2 * PACK]
             slope, gauss = row[2 * PACK : 3 * PACK], row[3 * PACK :]
-            for m in range(0, PATCH_SAMPLES, ROWS):
-                square = [squares[j, m : m + ROWS, :] for j in range(PACK)]
+            for m in range(0, PATCH_SAMPLES, STEP):
+                square = [squares[q * PACK + j, m : m + STEP, :] for j in range(PACK)]
                 below = [square[j] + half2[j] for j in range(PACK)]
                 above = list(lorentz)
                 while len(below) > 1:
@@ -202,16 +201,21 @@
                 value = above[0] / below[0]
                 for j in range(PACK):
                     value = value + gauss[j] * jnp.exp2(slope[j] * square[j])
-                mixed[m : m + ROWS, :] = value
-            for half in range(0, PATCH_SAMPLES, LANES):
-                turned = jnp.transpose(mixed[half : half + LANES, :])
-                summed = jnp.sum(turned.reshape(PACK, PIECE, LANES), axis=1)
-                tiles[t, q * PACK : (q + 1) * PACK, half : half + LANES] = summed
-            return carry
-
-        lax.fori_loop(0, THERMAL_SAMPLES, one, 0)
-
-    depth = plan.depth
+                high = value.astype(jnp.bfloat16)
+                low = (value - high.astype(f32)).astype(jnp.bfloat16)
+                mixed[m : m + STEP, 2 * q * LANES : (2 * q + 1) * LANES] = high
+                mixed[m : m + STEP, (2 * q + 1) * LANES : (2 * q + 2) * LANES] = low
+        tiles[t] = lax.dot_general(
+            seats,
+            mixed[...],
+            (((1,), (1,)), ((), ())),
+            preferred_element_type=f32,
+        )
+        return carry
+
+    lax.fori_loop(0, THERMAL_SAMPLES, one, 0, unroll=4)
+
+    depth = THERMAL_SAMPLES * SEATS
     column = lax.broadcasted_iota(jnp.int32, (blocks, depth), 1) % SEATS
     mine = rank_column == (column * temp_n).astype(f32) + me
     real = column < plan.share
@@ -226,64 +230,69 @@
 
     begins = jnp.concatenate(
         [begin[(n % PACK) * ROWS + n // PACK :][:1] for n in range(plan.quads * PACK)]
-        + [jnp.zeros((SEATS - plan.quads * PACK, LANES), f32)]
-    )
-    if plan.share < SEATS:
-        tiles[:, plan.share :, :] = jnp.zeros(
-            (THERMAL_SAMPLES, SEATS - plan.share, PATCH_SAMPLES), f32
+        + [jnp.zeros((SEATS - plan.quads * PACK, LANES), f32)] * (SEATS > plan.quads * PACK)
+    )
+    devices = plan.lines_n * temp_n
+    receiver = lax.broadcasted_iota(jnp.int32, (devices, depth), 0)
+    owner_place = (receiver // temp_n * plan.cap).astype(f32)
+    placed = [owner_place + slot == place_wide for slot in range(plan.cap)]
+    spread = []
+    for slot in range(plan.cap):
+        for order in range(plan.orders):
+            weight = jnp.concatenate([table[order]] * (devices // ROWS))
+            spread.append(jnp.where(placed[slot], weight, 0.0))
+    coefficients = jnp.dot(
+        jnp.concatenate(spread),
+        tiles[...].reshape(depth, PATCH_SAMPLES),
+        precision=HIGHEST,
+        preferred_element_type=f32,
+    )
+    for lot in range(plan.lots):
+        for half in range(2):
+            sent[pl.ds(2 * lot + half, devices, stride=plan.rows), :] = coefficients[
+                lot * devices : (lot + 1) * devices, half * LANES : (half + 1) * LANES
+            ]
+    held_lane = lax.broadcasted_iota(jnp.int32, (SEATS, LANES), 1) // PIECE
+    where_to = jnp.zeros((devices, LANES), f32)
+    for slot in range(plan.cap):
+        where_to = where_to + jnp.dot(
+            jnp.where(placed[slot][:, :SEATS], 1.0, 0.0),
+            jnp.where(held_lane == slot, begins, 0.0),
+            precision=HIGHEST,
+            preferred_element_type=f32,
         )
-    nothing = jnp.zeros_like(begins)
-    body = jnp.concatenate(
-        [
-            tiles[...].reshape(THERMAL_SAMPLES * SEATS, PATCH_SAMPLES),
-            jnp.concatenate([begins, nothing], axis=1),
-            jnp.concatenate([nothing, begins], axis=1),
-        ]
-    )
-    group = temp_n * plan.rows
-    weight, place = table[0], table[1]
-    for owner in range(plan.lines_n):
-        spread = jnp.where(
-            (place >= 0.0) & (place + owner * plan.cap == place_wide), weight, 0.0
-        )
-        sent[owner * group : (owner + 1) * group, :] = jnp.dot(
-            spread, body, precision=HIGHEST, preferred_element_type=f32
-        )
+    sent[pl.ds(2 * plan.lots, devices, stride=plan.rows), :] = where_to
 
 
 def place_kernel(plan, got, out):
     f32 = jnp.float32
     senders = plan.lines_n * plan.temp_n
     chunks = SPAN_SAMPLES // LANES
-    shape = (senders, plan.rows, LANES)
-    both = got[...].reshape(senders, plan.rows, PATCH_SAMPLES)
-    left, right = both[:, :, :LANES], both[:, :, LANES:]
-    sub = lax.broadcasted_iota(jnp.int32, shape, 1)
-    begin = jnp.zeros(shape, f32)
+    lane = lax.broadcasted_iota(jnp.int32, (senders, LANES), 1).astype(f32)
+
+    def take(row):
+        return got[pl.ds(row, senders, stride=plan.rows), :]
+
+    begins = take(2 * plan.lots)
+    hits, spread = [], []
     for slot in range(plan.cap):
-        row = plan.data_rows + slot // 2
-        source = (right if slot % 2 else left)[:, row : row + 1, :]
-        begin = jnp.where(sub // plan.orders == slot, source, begin)
-    chunk = jnp.floor(begin * (1.0 / LANES))
-    shift = begin - chunk * LANES
-    own = jnp.floor(chunk * (1.0 / chunks))
-    order = (sub % plan.orders).astype(f32)
-    target = (chunk - own * chunks) * ROWS + order * plan.held + own
-    lane = lax.broadcasted_iota(jnp.int32, shape, 2).astype(f32)
-    hit = jnp.where((sub < plan.data_rows) & (target == lane), 1.0, 0.0)
-    early = lane >= shift
-    rows = senders * plan.rows
-    spread = jnp.concatenate(
-        [
-            jnp.where(early, left, 0.0).reshape(rows, LANES),
-            right.reshape(rows, LANES),
-            jnp.where(early, 0.0, left).reshape(rows, LANES),
-        ],
-        axis=1,
-    )
+        begin = begins[:, slot * PIECE : slot * PIECE + 1]
+        chunk = jnp.floor(begin * (1.0 / LANES))
+        own = jnp.floor(chunk * (1.0 / chunks))
+        early = lane >= begin - chunk * LANES
+        target = (chunk - own * chunks) * ROWS + own
+        for order in range(plan.orders):
+            lot = slot * plan.orders + order
+            left, right = take(2 * lot), take(2 * lot + 1)
+            hits.append(jnp.where(target + order * plan.held == lane, 1.0, 0.0))
+            spread.append(
+                jnp.concatenate(
+                    [jnp.where(early, left, 0.0), right, jnp.where(early, 0.0, left)], axis=1
+                )
+            )
     landed = lax.dot_general(
-        hit.reshape(rows, LANES),
-        spread,
+        jnp.concatenate(hits),
+        jnp.concatenate(spread),
         (((0,), (0,)), ((), ())),
         precision=HIGHEST,
         preferred_element_type=f32,
@@ -322,11 +331,11 @@
     f32 = jnp.float32
     sent = pl.pallas_call(
         functools.partial(tile_kernel, plan),
-        out_shape=jax.ShapeDtypeStruct((devices * plan.rows, PATCH_SAMPLES), f32),
+        out_shape=pltpu.VMEM((devices * plan.rows, LANES), f32),
         scratch_shapes=[
             pltpu.VMEM((THERMAL_SAMPLES, 4 * PACK, ROWS, LANES), f32),
-            pltpu.VMEM((PACK, PATCH_SAMPLES, LANES), f32),
-            pltpu.VMEM((PATCH_SAMPLES, LANES), f32),
+            pltpu.VMEM((plan.quads * PACK, PATCH_SAMPLES, LANES), f32),
+            pltpu.VMEM((PATCH_SAMPLES, 2 * plan.quads * LANES), jnp.bfloat16),
             pltpu.VMEM((THERMAL_SAMPLES, SEATS, PATCH_SAMPLES), f32),
         ],
         name="tiles",
@@ -340,16 +349,16 @@
         block_window[None, :],
         tile_offset[None, :],
         owner_slot[None, :],
-        jnp.asarray(plan.tables()),
+        jnp.asarray(plan.table()),
     )
     got = lax.all_to_all(
-        sent.reshape(devices, plan.rows, PATCH_SAMPLES), ("lines", "temp"), 0, 0, tiled=True
+        sent.reshape(devices, 1, plan.rows * LANES), ("lines", "temp"), 0, 0, tiled=True
     )
     return pl.pallas_call(
         functools.partial(place_kernel, plan),
         out_shape=jax.ShapeDtypeStruct((plan.orders, plan.held, SPAN_SAMPLES), f32),
         name="place",
-    )(got.reshape(devices * plan.rows, PATCH_SAMPLES))
+    )(pltpu.with_memory_space_constraint(got.reshape(devices * plan.rows, LANES), pltpu.VMEM))
 
 
 def solution(mesh):

time: 29.1 us -> 24.1 us (0.83)
  Pallas kernels: 10.8 us -> 7.44 us
  blocking collectives: 18 us -> 16.5 us
    pallas_call x1, Pallas kernels: 8.77 us -> 6.29 us  [on_device(): pl.pallas_call(functools.partial(tile_kernel, plan), out_shape=pltpu.VMEM...]
    all_to_all x1, blocking collectives: 18 us -> 16.5 us  [on_device(): lax.all_to_all(sent.reshape(devices, 1, plan.rows * LANES), ('lines', 'te...]
    pallas_call x1, Pallas kernels: 2.07 us -> 1.15 us  [on_device(): pl.pallas_call(functools.partial(place_kernel, plan), out_shape=jax.Shape...]
where the time goes in v2:
time: 24.1 us; the launch traced here: 23.9 us
  blocking collectives  16.5 us (68%)
  Pallas kernels  7.44 us (31%)
    all_to_all x1, blocking collectives, on_device(): lax.all_to_all(sent.reshape(devices, 1, plan.rows * LANES), ('lines', 'te...  16.5 us
    pallas_call x1, Pallas kernels, on_device(): pl.pallas_call(functools.partial(tile_kernel, plan), out_shape=pltpu.VMEM...  6.29 us
    pallas_call x1, Pallas kernels, on_device(): pl.pallas_call(functools.partial(place_kernel, plan), out_shape=jax.Shape...  1.15 us

profile of v2, /device:TPU:0, one launch (start us, length us, event | category | flops | bytes accessed | tf_op | source)
XLA Modules:
  0.0 23.9 jit_solution(12411631539193462009)
XLA Ops:
  0.0 6.3 %tiles.1 = f32[416,128]{1,0:T(8,128)S(1)} custom-call(f32[48,128]{1,0:T(8,128)} %position.1, f32[48,128]{1,0:T(8,128)} %strength.1, f32[48,128]{1,0:T(8,128)} %energy.1, f32[48,128]{1,0:T(8,128)} %broad.1, f32[48,128]{1,0:T(8,128)} %power.1, f32[48,128]{1,0:T(8,128)} %doppler.1, s32[1,48]{1,0:T(1,128)} %bitcast.7, s32[1,48]{1,0:T(1,128)} %bitcast.8, ...), custom_call_target="tpu_custom_call" | custom-call | tf_op jit(solution)/shard_map/tiles/pallas_call | solution.py:332
  6.3 16.5 %all_to_all.5 = f32[32,1,1664]{2,1,0:T(1,128)S(1)} all-to-all(f32[32,1,1664]{2,1,0:T(1,128)S(1)} %bitcast.5), channel_id=1, replica_groups=mesh['lines'=8,'temp'=4] {'lines','temp'}, dimensions={0} | all-to-all | bytes 425984 | tf_op jit(solution)/shard_map/all_to_all | solution.py:354
  22.8 1.2 %place.1 = f32[2,4,2048]{2,1,0:T(4,128)} custom-call(f32[416,128]{1,0:T(8,128)S(1)} %bitcast.6), custom_call_target="tpu_custom_call" | custom-call | tf_op jit(solution)/shard_map/place/pallas_call | solution.py:357

commit v3 on v2

--- a/solution.py
+++ b/solution.py
@@ -15,9 +15,9 @@
 SPAN_SAMPLES = 2048
 THERMAL_SAMPLES = 8
 REFERENCE_KELVIN = 1000.0
-PACK = 4
-PIECE = LANES // PACK
+PIECE = 32
 SEATS = 16
+GROUP = 8
 STEP = 16
 HIGHEST = lax.Precision.HIGHEST
 
@@ -40,12 +40,16 @@
         self.held = spans // lines_n
         self.orders = THERMAL_SAMPLES // temp_n
         self.share = -(-blocks // temp_n)
-        self.quads = -(-self.share // PACK)
+        self.groups, first = [], 0
+        while first < self.share:
+            size = min(GROUP, 2 ** int(math.log2(self.share - first)))
+            self.groups.append((first, size))
+            first += size
         heavy = 3 * ((2 * blocks) // (3 * lines_n))
         self.cap = -(-heavy // temp_n)
         self.lots = self.cap * self.orders
         self.rows = 2 * self.lots + 1
-        assert self.share <= SEATS and self.cap <= PACK
+        assert self.share <= SEATS and self.cap <= LANES // PIECE and blocks % temp_n == 0
         assert self.orders * self.held <= ROWS and ROWS % temp_n == 0
 
     def table(self):
@@ -77,11 +81,26 @@
     narrow = 1.0 / full
     share = lw * narrow
     mixing = share * (1.36603 + share * (-0.47719 + share * 0.11116))
-    half = 0.5 * full
-    lorentz = scaled * mixing * half * (1.0 / math.pi)
-    gauss = scaled * (1.0 - mixing) * (0.939437 * narrow)
-    slope = (-2.7725887 * math.log2(math.e)) * narrow * narrow
-    return half * half, lorentz, slope, gauss
+    lorentz = (-2.0 / math.pi) * narrow * scaled * mixing
+    gauss = (2.0 * 0.939437) * narrow * scaled * (1.0 - mixing)
+    return -4.0 * narrow * narrow, lorentz, gauss
+
+
+def split(values, parts):
+    out = []
+    for part in range(parts):
+        out.append(values.astype(jnp.bfloat16))
+        if part < parts - 1:
+            values = values - out[-1].astype(jnp.float32)
+    return out
+
+
+def choose(ones, values, parts):
+    return jnp.dot(
+        jnp.concatenate([ones.astype(jnp.bfloat16)] * parts, axis=1),
+        jnp.concatenate(split(values, parts)),
+        preferred_element_type=jnp.float32,
+    )
 
 
 def tile_kernel(
@@ -101,6 +120,7 @@
     squares,
     mixed,
     tiles,
+    spread,
 ):
     blocks, temp_n = plan.blocks, plan.temp_n
     me = lax.axis_index("temp").astype(jnp.float32)
@@ -132,88 +152,42 @@
     rank_row = jnp.sum(jnp.where(key_column < key_row, 1.0, 0.0), axis=0, keepdims=True)
     rank_column = jnp.sum(jnp.where(key_row < key_column, 1.0, 0.0), axis=1, keepdims=True)
 
-    picks = PACK * ROWS
+    picks = len(plan.groups) * ROWS
     pick_row = lax.broadcasted_iota(jnp.int32, (picks, blocks), 0)
-    quad, piece = pick_row % ROWS, pick_row // ROWS
-    local = quad * PACK + piece
-    fits = (quad < plan.quads) & (local < plan.share)
-    wanted = jnp.where(fits, (local * temp_n).astype(f32) + me, 0.0)
-    pick = jnp.where(rank_row == wanted, 1.0, 0.0)
+    local = jnp.zeros((picks, blocks), jnp.int32)
+    for g, (first, size) in enumerate(plan.groups):
+        local = jnp.where(pick_row // ROWS == g, first + pick_row % size, local)
+    pick = jnp.where(rank_row == (local * temp_n).astype(f32) + me, 1.0, 0.0)
 
     def gather(values):
-        return jnp.dot(pick, values, precision=HIGHEST, preferred_element_type=f32)
-
+        return choose(pick, values, 3)
+
+    row = lax.broadcasted_iota(jnp.int32, (ROWS, LANES), 0)
     lane = lax.broadcasted_iota(jnp.int32, (ROWS, LANES), 1)
-    segment = lane // PIECE
 
     def pack(values):
-        parts = [values[i * ROWS : (i + 1) * ROWS] for i in range(PACK)]
         out = []
-        for j in range(PACK):
-            chosen = parts[0]
-            for i in range(1, PACK):
-                chosen = jnp.where(segment == (i + j) % PACK, parts[i], chosen)
-            out.append(chosen if j == 0 else pltpu.roll(chosen, LANES - j * PIECE, 1))
+        for g, (_, size) in enumerate(plan.groups):
+            part = values[g * ROWS : (g + 1) * ROWS]
+            width = LANES // size
+            for bit in range(size.bit_length() - 1):
+                step = 1 << bit
+                turned = pltpu.roll(part, ROWS - step, 0)
+                part = jnp.where(lane // width & step != 0, turned, part)
+            for bit in range(size.bit_length() - 1):
+                step = 1 << bit
+                turned = pltpu.roll(part, step * width, 1)
+                part = jnp.where(row & step != 0, turned, part)
+            out.append(part)
         return out
 
     begin = gather(jnp.broadcast_to(begin_column, (blocks, LANES)))
-    begin_packed = pack(begin)[0]
     columns = [pack(gather(r[...])) for r in (position, strength, energy, broad, power, doppler)]
-    for j in range(PACK):
+    begin_packed = pack(begin)
+    for g in range(len(plan.groups)):
         for t, kelvin in enumerate(kelvins()):
-            for k, value in enumerate(line_terms(*(c[j] for c in columns[1:]), kelvin)):
-                terms[t, k * PACK + j] = value
-
-    shift = begin_packed - jnp.floor(begin_packed * (1.0 / LANES)) * LANES
-    grid = iota((PATCH_SAMPLES, LANES), 0)
-    for q in range(plan.quads):
-        point = grid - shift[q : q + 1]
-        point = jnp.where(point < 0.0, point + PATCH_SAMPLES, point) + 0.5
-        for j in range(PACK):
-            distance = point - columns[0][j][q : q + 1]
-            squares[q * PACK + j] = distance * distance
-
-    width = 2 * plan.quads * LANES
-    across_lines = lax.broadcasted_iota(jnp.int32, (SEATS, width), 1)
-    seat_of = across_lines // (2 * LANES) * PACK + across_lines % LANES // PIECE
-    seats = jnp.where(
-        (seat_of == lax.broadcasted_iota(jnp.int32, (SEATS, width), 0)) & (seat_of < plan.share),
-        1.0,
-        0.0,
-    ).astype(jnp.bfloat16)
-
-    def one(t, carry):
-        for q in range(plan.quads):
-            row = [terms[t, k, pl.ds(q, 1), :] for k in range(4 * PACK)]
-            row = [jnp.broadcast_to(r, (STEP, LANES)) for r in row]
-            half2, lorentz = row[:PACK], row[PACK : 2 * PACK]
-            slope, gauss = row[2 * PACK : 3 * PACK], row[3 * PACK :]
-            for m in range(0, PATCH_SAMPLES, STEP):
-                square = [squares[q * PACK + j, m : m + STEP, :] for j in range(PACK)]
-                below = [square[j] + half2[j] for j in range(PACK)]
-                above = list(lorentz)
-                while len(below) > 1:
-                    above = [
-                        above[i] * below[i + 1] + above[i + 1] * below[i]
-                        for i in range(0, len(below), 2)
-                    ]
-                    below = [below[i] * below[i + 1] for i in range(0, len(below), 2)]
-                value = above[0] / below[0]
-                for j in range(PACK):
-                    value = value + gauss[j] * jnp.exp2(slope[j] * square[j])
-                high = value.astype(jnp.bfloat16)
-                low = (value - high.astype(f32)).astype(jnp.bfloat16)
-                mixed[m : m + STEP, 2 * q * LANES : (2 * q + 1) * LANES] = high
-                mixed[m : m + STEP, (2 * q + 1) * LANES : (2 * q + 2) * LANES] = low
-        tiles[t] = lax.dot_general(
-            seats,
-            mixed[...],
-            (((1,), (1,)), ((), ())),
-            preferred_element_type=f32,
-        )
-        return carry
-
-    lax.fori_loop(0, THERMAL_SAMPLES, one, 0, unroll=4)
+            for k, value in enumerate(line_terms(*(c[g] for c in columns[1:]), kelvin)):
+                terms[t, k, g * ROWS : (g + 1) * ROWS] = value
 
     depth = THERMAL_SAMPLES * SEATS
     column = lax.broadcasted_iota(jnp.int32, (blocks, depth), 1) % SEATS
@@ -229,20 +203,78 @@
     place_wide = jnp.where(column_row < plan.share, place_wide, -2.0)
 
     begins = jnp.concatenate(
-        [begin[(n % PACK) * ROWS + n // PACK :][:1] for n in range(plan.quads * PACK)]
-        + [jnp.zeros((SEATS - plan.quads * PACK, LANES), f32)] * (SEATS > plan.quads * PACK)
+        [begin[g * ROWS : g * ROWS + size] for g, (_, size) in enumerate(plan.groups)]
+        + [jnp.zeros((SEATS - plan.share, LANES), f32)] * (SEATS > plan.share)
     )
     devices = plan.lines_n * temp_n
     receiver = lax.broadcasted_iota(jnp.int32, (devices, depth), 0)
     owner_place = (receiver // temp_n * plan.cap).astype(f32)
     placed = [owner_place + slot == place_wide for slot in range(plan.cap)]
-    spread = []
     for slot in range(plan.cap):
         for order in range(plan.orders):
             weight = jnp.concatenate([table[order]] * (devices // ROWS))
-            spread.append(jnp.where(placed[slot], weight, 0.0))
+            lot = slot * plan.orders + order
+            spread[lot * devices : (lot + 1) * devices, :] = jnp.where(placed[slot], weight, 0.0)
+    held_lane = lax.broadcasted_iota(jnp.int32, (SEATS, LANES), 1) // PIECE
+    sent[pl.ds(2 * plan.lots, devices, stride=plan.rows), :] = choose(
+        jnp.concatenate([jnp.where(p[:, :SEATS], 1.0, 0.0) for p in placed], axis=1),
+        jnp.concatenate(
+            [jnp.where(held_lane == slot, begins, 0.0) for slot in range(plan.cap)]
+        ),
+        2,
+    )
+
+    grid = iota((PATCH_SAMPLES, LANES), 0)
+    for g, (first, size) in enumerate(plan.groups):
+        start = begin_packed[g][:1]
+        point = grid - (start - jnp.floor(start * (1.0 / LANES)) * LANES)
+        point = jnp.where(point < 0.0, point + PATCH_SAMPLES, point) + 0.5
+        for j in range(size):
+            distance = point - columns[0][g][j : j + 1]
+            squares[first + j] = distance * distance
+
+    width = 2 * LANES * len(plan.groups)
+    held_by = lax.broadcasted_iota(jnp.int32, (SEATS, width), 1)
+    seat_of = jnp.zeros((SEATS, width), jnp.int32)
+    for g, (first, size) in enumerate(plan.groups):
+        seat = first + held_by % LANES // (LANES // size)
+        seat_of = jnp.where(held_by // (2 * LANES) == g, seat, seat_of)
+    seats = jnp.where(
+        seat_of == lax.broadcasted_iota(jnp.int32, (SEATS, width), 0), 1.0, 0.0
+    ).astype(jnp.bfloat16)
+
+    def one(t, carry):
+        for g, (first, size) in enumerate(plan.groups):
+            rows = [
+                [
+                    jnp.broadcast_to(terms[t, k, g * ROWS + j : g * ROWS + j + 1, :], (STEP, LANES))
+                    for k in range(3)
+                ]
+                for j in range(size)
+            ]
+            for m in range(0, PATCH_SAMPLES, STEP):
+                value = None
+                for j, (scale, lorentz, gauss) in enumerate(rows):
+                    reach = squares[first + j, m : m + STEP, :] * scale - 1.0
+                    term = lorentz / reach + gauss * jnp.exp2(reach)
+                    value = term if value is None else value + term
+                high = value.astype(jnp.bfloat16)
+                low = (value - high.astype(f32)).astype(jnp.bfloat16)
+                mixed[m : m + STEP, 2 * g * LANES : (2 * g + 1) * LANES] = high
+                mixed[m : m + STEP, (2 * g + 1) * LANES : (2 * g + 2) * LANES] = low
+        for half in range(0, PATCH_SAMPLES, LANES):
+            tiles[t, :, half : half + LANES] = lax.dot_general(
+                seats,
+                mixed[half : half + LANES, :],
+                (((1,), (1,)), ((), ())),
+                preferred_element_type=f32,
+            )
+        return carry
+
+    lax.fori_loop(0, THERMAL_SAMPLES, one, 0, unroll=4)
+
     coefficients = jnp.dot(
-        jnp.concatenate(spread),
+        spread[...],
         tiles[...].reshape(depth, PATCH_SAMPLES),
         precision=HIGHEST,
         preferred_element_type=f32,
@@ -252,16 +284,6 @@
             sent[pl.ds(2 * lot + half, devices, stride=plan.rows), :] = coefficients[
                 lot * devices : (lot + 1) * devices, half * LANES : (half + 1) * LANES
             ]
-    held_lane = lax.broadcasted_iota(jnp.int32, (SEATS, LANES), 1) // PIECE
-    where_to = jnp.zeros((devices, LANES), f32)
-    for slot in range(plan.cap):
-        where_to = where_to + jnp.dot(
-            jnp.where(placed[slot][:, :SEATS], 1.0, 0.0),
-            jnp.where(held_lane == slot, begins, 0.0),
-            precision=HIGHEST,
-            preferred_element_type=f32,
-        )
-    sent[pl.ds(2 * plan.lots, devices, stride=plan.rows), :] = where_to
 
 
 def place_kernel(plan, got, out):
@@ -291,10 +313,9 @@
                 )
             )
     landed = lax.dot_general(
-        jnp.concatenate(hits),
-        jnp.concatenate(spread),
+        jnp.concatenate([jnp.concatenate(hits).astype(jnp.bfloat16)] * 3),
+        jnp.concatenate(split(jnp.concatenate(spread), 3)),
         (((0,), (0,)), ((), ())),
-        precision=HIGHEST,
         preferred_element_type=f32,
     )
     for c in range(chunks):
@@ -333,10 +354,11 @@
         functools.partial(tile_kernel, plan),
         out_shape=pltpu.VMEM((devices * plan.rows, LANES), f32),
         scratch_shapes=[
-            pltpu.VMEM((THERMAL_SAMPLES, 4 * PACK, ROWS, LANES), f32),
-            pltpu.VMEM((plan.quads * PACK, PATCH_SAMPLES, LANES), f32),
-            pltpu.VMEM((PATCH_SAMPLES, 2 * plan.quads * LANES), jnp.bfloat16),
+            pltpu.VMEM((THERMAL_SAMPLES, 3, len(plan.groups) * ROWS, LANES), f32),
+            pltpu.VMEM((plan.share, PATCH_SAMPLES, LANES), f32),
+            pltpu.VMEM((PATCH_SAMPLES, 2 * LANES * len(plan.groups)), jnp.bfloat16),
             pltpu.VMEM((THERMAL_SAMPLES, SEATS, PATCH_SAMPLES), f32),
+            pltpu.VMEM((plan.lots * devices, THERMAL_SAMPLES * SEATS), f32),
         ],
         name="tiles",
     )(

time: 24.1 us -> 23.4 us (0.971)
  Pallas kernels: 7.44 us -> 6.74 us
    pallas_call x1, Pallas kernels: 6.29 us -> 5.73 us  [on_device(): pl.pallas_call(functools.partial(tile_kernel, plan), out_shape=pltpu.VMEM...]
where the time goes in v3:
time: 23.4 us; the launch traced here: 23.2 us
  blocking collectives  16.5 us (71%)
  Pallas kernels  6.74 us (29%)
    all_to_all x1, blocking collectives, on_device(): lax.all_to_all(sent.reshape(devices, 1, plan.rows * LANES), ('lines', 'te...  16.5 us
    pallas_call x1, Pallas kernels, on_device(): pl.pallas_call(functools.partial(tile_kernel, plan), out_shape=pltpu.VMEM...  5.73 us
    pallas_call x1, Pallas kernels, on_device(): pl.pallas_call(functools.partial(place_kernel, plan), out_shape=jax.Shape...  1.01 us

profile of v3, /device:TPU:0, one launch (start us, length us, event | category | flops | bytes accessed | tf_op | source)
XLA Modules:
  0.0 23.2 jit_solution(9385151465896428271)
XLA Ops:
  0.0 5.7 %tiles.1 = f32[416,128]{1,0:T(8,128)S(1)} custom-call(f32[48,128]{1,0:T(8,128)} %position.1, f32[48,128]{1,0:T(8,128)} %strength.1, f32[48,128]{1,0:T(8,128)} %energy.1, f32[48,128]{1,0:T(8,128)} %broad.1, f32[48,128]{1,0:T(8,128)} %power.1, f32[48,128]{1,0:T(8,128)} %doppler.1, s32[1,48]{1,0:T(1,128)} %bitcast.7, s32[1,48]{1,0:T(1,128)} %bitcast.8, ...), custom_call_target="tpu_custom_call" | custom-call | tf_op jit(solution)/shard_map/tiles/pallas_call | solution.py:353
  5.7 16.5 %all_to_all.5 = f32[32,1,1664]{2,1,0:T(1,128)S(1)} all-to-all(f32[32,1,1664]{2,1,0:T(1,128)S(1)} %bitcast.5), channel_id=1, replica_groups=mesh['lines'=8,'temp'=4] {'lines','temp'}, dimensions={0} | all-to-all | bytes 425984 | tf_op jit(solution)/shard_map/all_to_all | solution.py:376
  22.2 1.0 %place.1 = f32[2,4,2048]{2,1,0:T(4,128)} custom-call(f32[416,128]{1,0:T(8,128)S(1)} %bitcast.6), custom_call_target="tpu_custom_call" | custom-call | tf_op jit(solution)/shard_map/place/pallas_call | solution.py:379

commit v4 on v3

--- a/solution.py
+++ b/solution.py
@@ -182,7 +182,9 @@
         return out
 
     begin = gather(jnp.broadcast_to(begin_column, (blocks, LANES)))
-    columns = [pack(gather(r[...])) for r in (position, strength, energy, broad, power, doppler)]
+    every = [r[...] for r in (position, strength, energy, broad, power, doppler)]
+    every = gather(jnp.concatenate(every, axis=1))
+    columns = [pack(every[:, i * LANES : (i + 1) * LANES]) for i in range(6)]
     begin_packed = pack(begin)
     for g in range(len(plan.groups)):
         for t, kelvin in enumerate(kelvins()):
@@ -214,7 +216,10 @@
         for order in range(plan.orders):
             weight = jnp.concatenate([table[order]] * (devices // ROWS))
             lot = slot * plan.orders + order
-            spread[lot * devices : (lot + 1) * devices, :] = jnp.where(placed[slot], weight, 0.0)
+            high, low = split(jnp.where(placed[slot], weight, 0.0), 2)
+            spread[lot * devices : (lot + 1) * devices, :] = jnp.concatenate(
+                [high, low, high], axis=1
+            )
     held_lane = lax.broadcasted_iota(jnp.int32, (SEATS, LANES), 1) // PIECE
     sent[pl.ds(2 * plan.lots, devices, stride=plan.rows), :] = choose(
         jnp.concatenate([jnp.where(p[:, :SEATS], 1.0, 0.0) for p in placed], axis=1),
@@ -244,28 +249,31 @@
     ).astype(jnp.bfloat16)
 
     def one(t, carry):
-        for g, (first, size) in enumerate(plan.groups):
-            rows = [
-                [
-                    jnp.broadcast_to(terms[t, k, g * ROWS + j : g * ROWS + j + 1, :], (STEP, LANES))
-                    for k in range(3)
+        part = PATCH_SAMPLES // 2
+        for half in range(0, PATCH_SAMPLES, part):
+            for g, (first, size) in enumerate(plan.groups):
+                rows = [
+                    [
+                        jnp.broadcast_to(
+                            terms[t, k, g * ROWS + j : g * ROWS + j + 1, :], (STEP, LANES)
+                        )
+                        for k in range(3)
+                    ]
+                    for j in range(size)
                 ]
-                for j in range(size)
-            ]
-            for m in range(0, PATCH_SAMPLES, STEP):
-                value = None
-                for j, (scale, lorentz, gauss) in enumerate(rows):
-                    reach = squares[first + j, m : m + STEP, :] * scale - 1.0
-                    term = lorentz / reach + gauss * jnp.exp2(reach)
-                    value = term if value is None else value + term
-                high = value.astype(jnp.bfloat16)
-                low = (value - high.astype(f32)).astype(jnp.bfloat16)
-                mixed[m : m + STEP, 2 * g * LANES : (2 * g + 1) * LANES] = high
-                mixed[m : m + STEP, (2 * g + 1) * LANES : (2 * g + 2) * LANES] = low
-        for half in range(0, PATCH_SAMPLES, LANES):
-            tiles[t, :, half : half + LANES] = lax.dot_general(
+                for m in range(half, half + part, STEP):
+                    lorentz_sum, gauss_sum = None, None
+                    for j, (scale, lorentz, gauss) in enumerate(rows):
+                        reach = squares[first + j, m : m + STEP, :] * scale - 1.0
+                        one_l, one_g = lorentz / reach, gauss * jnp.exp2(reach)
+                        lorentz_sum = one_l if j == 0 else lorentz_sum + one_l
+                        gauss_sum = one_g if j == 0 else gauss_sum + one_g
+                    high, low = split(lorentz_sum + gauss_sum, 2)
+                    mixed[m : m + STEP, 2 * g * LANES : (2 * g + 1) * LANES] = high
+                    mixed[m : m + STEP, (2 * g + 1) * LANES : (2 * g + 2) * LANES] = low
+            tiles[t, :, half : half + part] = lax.dot_general(
                 seats,
-                mixed[half : half + LANES, :],
+                mixed[half : half + part, :],
                 (((1,), (1,)), ((), ())),
                 preferred_element_type=f32,
             )
@@ -273,11 +281,9 @@
 
     lax.fori_loop(0, THERMAL_SAMPLES, one, 0, unroll=4)
 
+    high, low = split(tiles[...].reshape(depth, PATCH_SAMPLES), 2)
     coefficients = jnp.dot(
-        spread[...],
-        tiles[...].reshape(depth, PATCH_SAMPLES),
-        precision=HIGHEST,
-        preferred_element_type=f32,
+        spread[...], jnp.concatenate([high, high, low]), preferred_element_type=f32
     )
     for lot in range(plan.lots):
         for half in range(2):
@@ -313,11 +319,12 @@
                 )
             )
     landed = lax.dot_general(
-        jnp.concatenate([jnp.concatenate(hits).astype(jnp.bfloat16)] * 3),
-        jnp.concatenate(split(jnp.concatenate(spread), 3)),
+        jnp.concatenate(hits).astype(jnp.bfloat16),
+        jnp.concatenate(split(jnp.concatenate(spread), 3), axis=1),
         (((0,), (0,)), ((), ())),
         preferred_element_type=f32,
     )
+    landed = landed[:, : 3 * LANES] + landed[:, 3 * LANES : 6 * LANES] + landed[:, 6 * LANES :]
     for c in range(chunks):
         total = landed[c * ROWS : (c + 1) * ROWS, :LANES]
         for back in (1, 2):
@@ -358,7 +365,7 @@
             pltpu.VMEM((plan.share, PATCH_SAMPLES, LANES), f32),
             pltpu.VMEM((PATCH_SAMPLES, 2 * LANES * len(plan.groups)), jnp.bfloat16),
             pltpu.VMEM((THERMAL_SAMPLES, SEATS, PATCH_SAMPLES), f32),
-            pltpu.VMEM((plan.lots * devices, THERMAL_SAMPLES * SEATS), f32),
+            pltpu.VMEM((plan.lots * devices, 3 * THERMAL_SAMPLES * SEATS), jnp.bfloat16),
         ],
         name="tiles",
     )(

time: 23.4 us -> 23.3 us (level)
  no operation moved by 1% of the time
where the time goes in v4:
time: 23.3 us; the launch traced here: 23.1 us
  blocking collectives  16.5 us (71%)
  Pallas kernels  6.61 us (28%)
    all_to_all x1, blocking collectives, on_device(): lax.all_to_all(sent.reshape(devices, 1, plan.rows * LANES), ('lines', 'te...  16.5 us
    pallas_call x1, Pallas kernels, on_device(): pl.pallas_call(functools.partial(tile_kernel, plan), out_shape=pltpu.VMEM...  5.61 us
    pallas_call x1, Pallas kernels, on_device(): pl.pallas_call(functools.partial(place_kernel, plan), out_shape=jax.Shape...  1.01 us

profile of v4, /device:TPU:0, one launch (start us, length us, event | category | flops | bytes accessed | tf_op | source)
XLA Modules:
  0.0 23.1 jit_solution(10126191574018451509)
XLA Ops:
  0.0 5.6 %tiles.1 = f32[416,128]{1,0:T(8,128)S(1)} custom-call(f32[48,128]{1,0:T(8,128)} %position.1, f32[48,128]{1,0:T(8,128)} %strength.1, f32[48,128]{1,0:T(8,128)} %energy.1, f32[48,128]{1,0:T(8,128)} %broad.1, f32[48,128]{1,0:T(8,128)} %power.1, f32[48,128]{1,0:T(8,128)} %doppler.1, s32[1,48]{1,0:T(1,128)} %bitcast.7, s32[1,48]{1,0:T(1,128)} %bitcast.8, ...), custom_call_target="tpu_custom_call" | custom-call | tf_op jit(solution)/shard_map/tiles/pallas_call | solution.py:360
  5.6 16.5 %all_to_all.5 = f32[32,1,1664]{2,1,0:T(1,128)S(1)} all-to-all(f32[32,1,1664]{2,1,0:T(1,128)S(1)} %bitcast.5), channel_id=1, replica_groups=mesh['lines'=8,'temp'=4] {'lines','temp'}, dimensions={0} | all-to-all | bytes 425984 | tf_op jit(solution)/shard_map/all_to_all | solution.py:383
  22.1 1.0 %place.1 = f32[2,4,2048]{2,1,0:T(4,128)} custom-call(f32[416,128]{1,0:T(8,128)S(1)} %bitcast.6), custom_call_target="tpu_custom_call" | custom-call | tf_op jit(solution)/shard_map/place/pallas_call | solution.py:386

commit v5 on v4

--- a/solution.py
+++ b/solution.py
@@ -84,6 +84,14 @@
     lorentz = (-2.0 / math.pi) * narrow * scaled * mixing
     gauss = (2.0 * 0.939437) * narrow * scaled * (1.0 - mixing)
     return -4.0 * narrow * narrow, lorentz, gauss
+
+
+def quotient(values, power):
+    return lax.shift_right_logical(values, jnp.int32(power.bit_length() - 1))
+
+
+def remainder(values, power):
+    return values & (power - 1)
 
 
 def split(values, parts):
@@ -152,11 +160,14 @@
     rank_row = jnp.sum(jnp.where(key_column < key_row, 1.0, 0.0), axis=0, keepdims=True)
     rank_column = jnp.sum(jnp.where(key_row < key_column, 1.0, 0.0), axis=1, keepdims=True)
 
-    picks = len(plan.groups) * ROWS
-    pick_row = lax.broadcasted_iota(jnp.int32, (picks, blocks), 0)
-    local = jnp.zeros((picks, blocks), jnp.int32)
-    for g, (first, size) in enumerate(plan.groups):
-        local = jnp.where(pick_row // ROWS == g, first + pick_row % size, local)
+    spans = [size * ROWS for _, size in plan.groups]
+    starts = [sum(spans[:g]) for g in range(len(spans))]
+    pick_row = lax.broadcasted_iota(jnp.int32, (sum(spans), blocks), 0)
+    local = jnp.zeros((sum(spans), blocks), jnp.int32)
+    for (first, size), start in zip(plan.groups, starts):
+        turned = pick_row - start
+        turned = first + remainder(quotient(turned, ROWS) + turned, size)
+        local = jnp.where(pick_row >= start, turned, local)
     pick = jnp.where(rank_row == (local * temp_n).astype(f32) + me, 1.0, 0.0)
 
     def gather(values):
@@ -167,17 +178,19 @@
 
     def pack(values):
         out = []
-        for g, (_, size) in enumerate(plan.groups):
-            part = values[g * ROWS : (g + 1) * ROWS]
+        for (_, size), start in zip(plan.groups, starts):
             width = LANES // size
-            for bit in range(size.bit_length() - 1):
-                step = 1 << bit
-                turned = pltpu.roll(part, ROWS - step, 0)
-                part = jnp.where(lane // width & step != 0, turned, part)
-            for bit in range(size.bit_length() - 1):
-                step = 1 << bit
-                turned = pltpu.roll(part, step * width, 1)
-                part = jnp.where(row & step != 0, turned, part)
+            part = values[start : start + ROWS]
+            for turn in range(1, size):
+                turned = values[start + turn * ROWS : start + (turn + 1) * ROWS]
+                part = jnp.where(quotient(lane, width) == turn, turned, part)
+            if size == ROWS:
+                part = pltpu.roll(part, 0, 1, stride=width, stride_axis=0)
+            else:
+                for bit in range(size.bit_length() - 1):
+                    step = 1 << bit
+                    turned = pltpu.roll(part, step * width, 1)
+                    part = jnp.where(row & step != 0, turned, part)
             out.append(part)
         return out
 
@@ -192,25 +205,25 @@
                 terms[t, k, g * ROWS : (g + 1) * ROWS] = value
 
     depth = THERMAL_SAMPLES * SEATS
-    column = lax.broadcasted_iota(jnp.int32, (blocks, depth), 1) % SEATS
+    column = remainder(lax.broadcasted_iota(jnp.int32, (blocks, depth), 1), SEATS)
     mine = rank_column == (column * temp_n).astype(f32) + me
     real = column < plan.share
     owner_wide = jnp.sum(jnp.where(mine & real, owner_column, 0.0), axis=0, keepdims=True)
     first_wide = jnp.sum(
         jnp.where(owner_column < owner_wide, 1.0, 0.0), axis=0, keepdims=True
     )
-    column_row = lax.broadcasted_iota(jnp.int32, (1, depth), 1) % SEATS
+    column_row = remainder(lax.broadcasted_iota(jnp.int32, (1, depth), 1), SEATS)
     skipped = jnp.floor((first_wide - me + (temp_n - 0.5)) * (1.0 / temp_n))
     place_wide = owner_wide * plan.cap + column_row.astype(f32) - skipped
     place_wide = jnp.where(column_row < plan.share, place_wide, -2.0)
 
     begins = jnp.concatenate(
-        [begin[g * ROWS : g * ROWS + size] for g, (_, size) in enumerate(plan.groups)]
+        [begin[start : start + size] for (_, size), start in zip(plan.groups, starts)]
         + [jnp.zeros((SEATS - plan.share, LANES), f32)] * (SEATS > plan.share)
     )
     devices = plan.lines_n * temp_n
     receiver = lax.broadcasted_iota(jnp.int32, (devices, depth), 0)
-    owner_place = (receiver // temp_n * plan.cap).astype(f32)
+    owner_place = (quotient(receiver, temp_n) * plan.cap).astype(f32)
     placed = [owner_place + slot == place_wide for slot in range(plan.cap)]
     for slot in range(plan.cap):
         for order in range(plan.orders):
@@ -220,7 +233,7 @@
             spread[lot * devices : (lot + 1) * devices, :] = jnp.concatenate(
                 [high, low, high], axis=1
             )
-    held_lane = lax.broadcasted_iota(jnp.int32, (SEATS, LANES), 1) // PIECE
+    held_lane = quotient(lax.broadcasted_iota(jnp.int32, (SEATS, LANES), 1), PIECE)
     sent[pl.ds(2 * plan.lots, devices, stride=plan.rows), :] = choose(
         jnp.concatenate([jnp.where(p[:, :SEATS], 1.0, 0.0) for p in placed], axis=1),
         jnp.concatenate(
@@ -242,8 +255,8 @@
     held_by = lax.broadcasted_iota(jnp.int32, (SEATS, width), 1)
     seat_of = jnp.zeros((SEATS, width), jnp.int32)
     for g, (first, size) in enumerate(plan.groups):
-        seat = first + held_by % LANES // (LANES // size)
-        seat_of = jnp.where(held_by // (2 * LANES) == g, seat, seat_of)
+        seat = first + quotient(remainder(held_by, LANES), LANES // size)
+        seat_of = jnp.where(quotient(held_by, 2 * LANES) == g, seat, seat_of)
     seats = jnp.where(
         seat_of == lax.broadcasted_iota(jnp.int32, (SEATS, width), 0), 1.0, 0.0
     ).astype(jnp.bfloat16)

time: 23.3 us -> 23.3 us (level)
  no operation moved by 1% of the time
where the time goes in v5:
time: 23.3 us; the launch traced here: 23.1 us
  blocking collectives  16.5 us (71%)
  Pallas kernels  6.6 us (28%)
    all_to_all x1, blocking collectives, on_device(): lax.all_to_all(sent.reshape(devices, 1, plan.rows * LANES), ('lines', 'te...  16.5 us
    pallas_call x1, Pallas kernels, on_device(): pl.pallas_call(functools.partial(tile_kernel, plan), out_shape=pltpu.VMEM...  5.59 us
    pallas_call x1, Pallas kernels, on_device(): pl.pallas_call(functools.partial(place_kernel, plan), out_shape=jax.Shape...  1.01 us

profile of v5, /device:TPU:0, one launch (start us, length us, event | category | flops | bytes accessed | tf_op | source)
XLA Modules:
  0.0 23.1 jit_solution(17083873276680304988)
XLA Ops:
  0.0 5.6 %tiles.1 = f32[416,128]{1,0:T(8,128)S(1)} custom-call(f32[48,128]{1,0:T(8,128)} %position.1, f32[48,128]{1,0:T(8,128)} %strength.1, f32[48,128]{1,0:T(8,128)} %energy.1, f32[48,128]{1,0:T(8,128)} %broad.1, f32[48,128]{1,0:T(8,128)} %power.1, f32[48,128]{1,0:T(8,128)} %doppler.1, s32[1,48]{1,0:T(1,128)} %bitcast.7, s32[1,48]{1,0:T(1,128)} %bitcast.8, ...), custom_call_target="tpu_custom_call" | custom-call | tf_op jit(solution)/shard_map/tiles/pallas_call | solution.py:373
  5.6 16.5 %all_to_all.5 = f32[32,1,1664]{2,1,0:T(1,128)S(1)} all-to-all(f32[32,1,1664]{2,1,0:T(1,128)S(1)} %bitcast.5), channel_id=1, replica_groups=mesh['lines'=8,'temp'=4] {'lines','temp'}, dimensions={0} | all-to-all | bytes 425984 | tf_op jit(solution)/shard_map/all_to_all | solution.py:396
  22.1 1.0 %place.1 = f32[2,4,2048]{2,1,0:T(4,128)} custom-call(f32[416,128]{1,0:T(8,128)S(1)} %bitcast.6), custom_call_target="tpu_custom_call" | custom-call | tf_op jit(solution)/shard_map/place/pallas_call | solution.py:399

commit v6 on v5

--- a/solution.py
+++ b/solution.py
@@ -19,7 +19,6 @@
 SEATS = 16
 GROUP = 8
 STEP = 16
-HIGHEST = lax.Precision.HIGHEST
 
 
 def kelvins():
@@ -137,8 +136,7 @@
     def iota(shape, axis):
         return lax.broadcasted_iota(jnp.int32, shape, axis).astype(f32)
 
-    down, across = iota((blocks, blocks), 0), iota((blocks, blocks), 1)
-    eye = down == across
+    eye = iota((blocks, blocks), 0) == iota((blocks, blocks), 1)
 
     def stand(row):
         return jnp.sum(jnp.where(eye, row, 0.0), axis=1, keepdims=True)
@@ -268,20 +266,22 @@
                 rows = [
                     [
                         jnp.broadcast_to(
-                            terms[t, k, g * ROWS + j : g * ROWS + j + 1, :], (STEP, LANES)
+                            terms[t, k, g * ROWS + j : g * ROWS + j + 1, :], (ROWS, LANES)
                         )
                         for k in range(3)
                     ]
                     for j in range(size)
                 ]
                 for m in range(half, half + part, STEP):
-                    lorentz_sum, gauss_sum = None, None
-                    for j, (scale, lorentz, gauss) in enumerate(rows):
-                        reach = squares[first + j, m : m + STEP, :] * scale - 1.0
-                        one_l, one_g = lorentz / reach, gauss * jnp.exp2(reach)
-                        lorentz_sum = one_l if j == 0 else lorentz_sum + one_l
-                        gauss_sum = one_g if j == 0 else gauss_sum + one_g
-                    high, low = split(lorentz_sum + gauss_sum, 2)
+                    sums = []
+                    for at in range(m, m + STEP, ROWS):
+                        total = None
+                        for j, (scale, lorentz, gauss) in enumerate(rows):
+                            reach = squares[first + j, at : at + ROWS, :] * scale - 1.0
+                            term = lorentz / reach + gauss * jnp.exp2(reach)
+                            total = term if j == 0 else total + term
+                        sums.append(total)
+                    high, low = split(jnp.concatenate(sums), 2)
                     mixed[m : m + STEP, 2 * g * LANES : (2 * g + 1) * LANES] = high
                     mixed[m : m + STEP, (2 * g + 1) * LANES : (2 * g + 2) * LANES] = low
             tiles[t, :, half : half + part] = lax.dot_general(
@@ -331,13 +331,12 @@
                     [jnp.where(early, left, 0.0), right, jnp.where(early, 0.0, left)], axis=1
                 )
             )
-    landed = lax.dot_general(
-        jnp.concatenate(hits).astype(jnp.bfloat16),
-        jnp.concatenate(split(jnp.concatenate(spread), 3), axis=1),
-        (((0,), (0,)), ((), ())),
+    landed = jnp.dot(
+        jnp.transpose(jnp.concatenate(hits)).astype(jnp.bfloat16),
+        jnp.concatenate(split(jnp.concatenate(spread), 2), axis=1),
         preferred_element_type=f32,
     )
-    landed = landed[:, : 3 * LANES] + landed[:, 3 * LANES : 6 * LANES] + landed[:, 6 * LANES :]
+    landed = landed[:, : 3 * LANES] + landed[:, 3 * LANES :]
     for c in range(chunks):
         total = landed[c * ROWS : (c + 1) * ROWS, :LANES]
         for back in (1, 2):

time: 23.3 us -> 23.2 us (level)
  no operation moved by 1% of the time
where the time goes in v6:
time: 23.2 us; the launch traced here: 23 us
  blocking collectives  16.5 us (71%)
  Pallas kernels  6.53 us (28%)
    all_to_all x1, blocking collectives, on_device(): lax.all_to_all(sent.reshape(devices, 1, plan.rows * LANES), ('lines', 'te...  16.5 us
    pallas_call x1, Pallas kernels, on_device(): pl.pallas_call(functools.partial(tile_kernel, plan), out_shape=pltpu.VMEM...  5.55 us
    pallas_call x1, Pallas kernels, on_device(): pl.pallas_call(functools.partial(place_kernel, plan), out_shape=jax.Shape...  0.98 us

profile of v6, /device:TPU:0, one launch (start us, length us, event | category | flops | bytes accessed | tf_op | source)
XLA Modules:
  0.0 23.0 jit_solution(5414368262162269406)
XLA Ops:
  0.0 5.5 %tiles.1 = f32[416,128]{1,0:T(8,128)S(1)} custom-call(f32[48,128]{1,0:T(8,128)} %position.1, f32[48,128]{1,0:T(8,128)} %strength.1, f32[48,128]{1,0:T(8,128)} %energy.1, f32[48,128]{1,0:T(8,128)} %broad.1, f32[48,128]{1,0:T(8,128)} %power.1, f32[48,128]{1,0:T(8,128)} %doppler.1, s32[1,48]{1,0:T(1,128)} %bitcast.7, s32[1,48]{1,0:T(1,128)} %bitcast.8, ...), custom_call_target="tpu_custom_call" | custom-call | tf_op jit(solution)/shard_map/tiles/pallas_call | solution.py:372
  5.6 16.5 %all_to_all.5 = f32[32,1,1664]{2,1,0:T(1,128)S(1)} all-to-all(f32[32,1,1664]{2,1,0:T(1,128)S(1)} %bitcast.5), channel_id=1, replica_groups=mesh['lines'=8,'temp'=4] {'lines','temp'}, dimensions={0} | all-to-all | bytes 425984 | tf_op jit(solution)/shard_map/all_to_all | solution.py:395
  22.0 1.0 %place.1 = f32[2,4,2048]{2,1,0:T(4,128)} custom-call(f32[416,128]{1,0:T(8,128)S(1)} %bitcast.6), custom_call_target="tpu_custom_call" | custom-call | tf_op jit(solution)/shard_map/place/pallas_call | solution.py:398
